TPU v7x, 32 devices: a whole 2x2x4 slice. The times are simulated.
32 devices in a mesh: obs: 8 (over z, core), state: 4 (over y, x).
Axes of the slice: x: 2, y: 2, z: 4, core: 2. Of those that a mesh axis runs over, the one named last changes fastest.
Arguments:
- ensemble: bfloat16 [4, 1024, 256], P('state'), may hold values from -16 to 16
- obs_values: float32 [16384], P('obs'), may hold values from -72 to 72
- obs_error: float32 [16384], P('obs'), may hold values from 6 to 24
- h_blocks: bfloat16 [8, 4, 64, 128, 128], P('obs', 'state'), may hold values from -0.125 to 0.125
- block_rows: int32 [8, 4, 64], P('obs', 'state'), may hold values from 0 to 15
- block_cols: int32 [8, 4, 64], P('obs', 'state'), may hold values from 0 to 7
- block_count: int32 [8, 4], P('obs', 'state'), may hold values from 32 to 64, as said below
Outputs:
- analysis: bfloat16 [4, 1024, 256], P('state', 'obs')
Inputs may be any that keep to these rules, and one draw needn't show every extreme that they name: `block_count`: some device has exactly 64 live slots in every draw.
All inputs are finite; a program needn't handle non-finite values.
Results may differ from a plain program's by a relative error of at most 0.009.
Values sent between devices are 32-bit elements; how exact they have to be, the bound alone decides.
A program may use at most 64 MiB of HBM per device.

v0:
```python
import math
import jax
import jax.numpy as jnp
from jax import lax
from jax.sharding import PartitionSpec as P

K = 256
BS = 128
M_DEV = 2048
BLK_DEV = 64


def on_device(ensemble, obs_values, obs_error, h_blocks, block_rows, block_cols, block_count):
    members = ensemble[0]
    slab_rows = members.shape[0]
    state_blocks = slab_rows // BS
    obs_blocks = M_DEV // BS
    member_blocks = members.reshape(state_blocks, BS, K)
    group_size = math.gcd(BLK_DEV, 32)
    group_count = BLK_DEV // group_size
    all_blocks = h_blocks[0, 0]
    all_cols = block_cols[0, 0]
    all_rows = block_rows[0, 0]
    live_count = block_count[0, 0]
    block_ids = jnp.arange(obs_blocks, dtype=jnp.int32)

    def add_group(group_index, carry):
        start = (group_index * group_size).astype(jnp.int32)
        blocks = lax.dynamic_slice_in_dim(all_blocks, start, group_size, 0)
        cols = lax.dynamic_slice_in_dim(all_cols, start, group_size, 0)
        rows = lax.dynamic_slice_in_dim(all_rows, start, group_size, 0)
        live_mask = start + jnp.arange(group_size, dtype=jnp.int32) < live_count
        picked = member_blocks[cols]
        products = jnp.einsum("bij,bjk->bik", blocks, picked, preferred_element_type=jnp.float32)
        upper_part = products.astype(jnp.bfloat16)
        lower_part = (products - upper_part.astype(jnp.float32)).astype(jnp.bfloat16)
        onehot = ((rows[None, :] == block_ids[:, None]) & live_mask[None, :]).astype(jnp.bfloat16)
        carry = carry + jnp.einsum(
            "mb,bik->mik", onehot, upper_part, preferred_element_type=jnp.float32
        )
        carry = carry + jnp.einsum(
            "mb,bik->mik", onehot, lower_part, preferred_element_type=jnp.float32
        )
        return carry

    accumulated = lax.fori_loop(
        0, group_count, add_group, jnp.zeros((obs_blocks, BS, K), jnp.float32)
    )
    slab_term = accumulated.reshape(M_DEV, K)
    state_devices = lax.axis_size("state")
    rows_share = M_DEV // state_devices
    row_offset = lax.axis_index("state") * rows_share
    own_rows = lax.psum_scatter(slab_term, "state", scatter_dimension=0, tiled=True)
    own_values = lax.dynamic_slice_in_dim(obs_values, row_offset, rows_share, 0)
    own_errors = lax.dynamic_slice_in_dim(obs_error, row_offset, rows_share, 0)
    obs_mean = jnp.mean(own_rows, axis=1)
    whitened = (own_rows - obs_mean[:, None]) / own_errors[:, None]
    innovation = (own_values - obs_mean) / own_errors
    gram_part = lax.dot_general(
        whitened, whitened, (((0,), (0,)), ((), ())), precision=lax.Precision.HIGHEST
    )
    projected_part = jnp.dot(innovation, whitened, precision=lax.Precision.HIGHEST)
    identity = jnp.eye(K, dtype=jnp.float32)
    gram_sum, projected_innovation = lax.psum((gram_part, projected_part), ("obs", "state"))
    lower_factor = jnp.linalg.cholesky(gram_sum + (K - 1) * identity)
    halfway = lax.linalg.triangular_solve(
        lower_factor, projected_innovation[:, None], left_side=True, lower=True
    )
    mean_weight = lax.linalg.triangular_solve(
        lower_factor, halfway, left_side=True, lower=True, transpose_a=True
    )
    root_inverse = lax.linalg.triangular_solve(
        lower_factor, identity, left_side=True, lower=True, transpose_a=True
    )
    transform = (math.sqrt(K - 1) * root_inverse + mean_weight).astype(jnp.bfloat16)
    piece_rows = slab_rows // lax.axis_size("obs")
    own_piece = lax.dynamic_slice_in_dim(
        members, lax.axis_index("obs") * piece_rows, piece_rows, 0
    ).astype(jnp.float32)
    state_mean = jnp.mean(own_piece, axis=1)
    anomalies = (own_piece - state_mean[:, None]).astype(jnp.bfloat16)
    analysis = state_mean[:, None] + jnp.dot(
        anomalies, transform, preferred_element_type=jnp.float32
    )
    return analysis.astype(jnp.bfloat16)[None]


def solution(mesh):
    placed = (
        P("state", None, None),
        P("obs"),
        P("obs"),
        P("obs", "state", None, None, None),
        P("obs", "state", None),
        P("obs", "state", None),
        P("obs", "state"),
    )
    return jax.shard_map(
        on_device, mesh=mesh, in_specs=placed, out_specs=P("state", "obs", None), check_vma=False
    )
```

profile of v0, /device:TPU:0, one launch (start us, length us, event | category | flops | bytes accessed | tf_op | source)
XLA Modules:
  0.0 278.9 jit_solution(10647405630408804250)
XLA Ops:
  6.5 24.7 %while.16 = (s32[]{:T(128)}, f32[16,128,256]{2,0,1:T(8,128)}, s32[64]{0:T(128)}, s32[]{:T(128)}, bf16[64,128,128]{2,1,0:T(8,128)(2,1)}, /*index=5*/s32[64]{0:T(1...) while((s32[]{:T(128)}, f32[16,128,256]{2,0,1:T(8,128)}, ...), condition=%wide.region_2.0_spmd.clone, body=%wide.region_1.0_spmd.clone.sunk | while | flops 341314720 | bytes 24123700 | solution.py:46
  6.5 0.7 compare_select_fusion.2
  7.3 1.7 gather_fusion
  9.0 3.2 %subtract_convert_fusion.2 = (bf16[32,128,256]{2,1,0:T(8,128)(2,1)S(1)}, bf16[32,128,256]{2,1,0:T(8,128)(2,1)}) fusion(bf16[32,128,256]{2,1,0:T(8,128)(2,1)S(1)} %gather_fusion, bf16[64,128,128]{2,1,0:T(8,128)(2,1)} %get-tuple-element.322, s32[]{:T(128)S(6)} %select_n.37), kind=kOutput, calls=%fused_computation.4.clone.1 | convolution fusion | flops 272629760 | bytes 7340036 | tf_op jit(solution)/shard_map/while/body/eval_jaxpr/bij,bjk->bik/dot_general | solution.py:34
  13.0 1.3 fusion.80
  14.2 4.3 %fusion.81 = f32[16,128,256]{2,0,1:T(8,128)} fusion(f32[16,128,256]{2,0,1:T(8,128)S(1)} %fusion.80, f32[16,128,256]{2,0,1:T(8,128)} %get-tuple-element.308, bf16[32,128,256]{2,1,0:T(8,128)(2,1)} %get-tuple-element.295, pred[]{:T(512)S(6)} %compare.30, s32[32]{0:T(128)S(1)} %dynamic_slice.54, pred[32]{0:T(512)(128)(4,1)S(1)} %add_compare_fusion.2), kind=kOutput, calls=%fused_computation.10.clone.1 | convolution fusion | flops 35128320 | bytes 8388769 | tf_op jit(solution)/shard_map/while/body/eval_jaxpr/mb,bik->mik/dot_general | solution.py:38
  18.6 0.7 compare_select_fusion.2
  19.3 1.7 gather_fusion
  21.0 3.2 %subtract_convert_fusion.2 = (bf16[32,128,256]{2,1,0:T(8,128)(2,1)S(1)}, bf16[32,128,256]{2,1,0:T(8,128)(2,1)}) fusion(bf16[32,128,256]{2,1,0:T(8,128)(2,1)S(1)} %gather_fusion, bf16[64,128,128]{2,1,0:T(8,128)(2,1)} %get-tuple-element.322, s32[]{:T(128)S(6)} %select_n.37), kind=kOutput, calls=%fused_computation.4.clone.1 | convolution fusion | flops 272629760 | bytes 7340036 | tf_op jit(solution)/shard_map/while/body/eval_jaxpr/bij,bjk->bik/dot_general | solution.py:34
  25.0 1.3 fusion.80
  26.3 5.0 %fusion.81 = f32[16,128,256]{2,0,1:T(8,128)} fusion(f32[16,128,256]{2,0,1:T(8,128)S(1)} %fusion.80, f32[16,128,256]{2,0,1:T(8,128)} %get-tuple-element.308, bf16[32,128,256]{2,1,0:T(8,128)(2,1)} %get-tuple-element.295, pred[]{:T(512)S(6)} %compare.30, s32[32]{0:T(128)S(1)} %dynamic_slice.54, pred[32]{0:T(512)(128)(4,1)S(1)} %add_compare_fusion.2), kind=kOutput, calls=%fused_computation.10.clone.1 | convolution fusion | flops 35128320 | bytes 8388769 | tf_op jit(solution)/shard_map/while/body/eval_jaxpr/mb,bik->mik/dot_general | solution.py:38
  31.2 4.1 %copy.18 = f32[16,128,256]{2,1,0:T(8,128)} copy(f32[16,128,256]{2,0,1:T(8,128)} %get-tuple-element.144) | data formatting | bytes 4194304 | tf_op jit(solution)/shard_map/while | solution.py:46
  35.4 0.9 convert_reduce_fusion
  36.4 37.0 %reduce-scatter.2.cloned.1.call-done = f32[512,256]{1,0:T(8,128)} async-done(((f32[2048,256]{1,0:T(8,128)}), f32[512,256]{1,0:T(8,128)}) %reduce-scatter.2.cloned.1.call-update) | async-done | bytes 524304 | tf_op jit(solution)/shard_map/reduce_scatter | solution.py:53
  73.4 1.3 reduce_sum.19
  74.7 0.8 subtract_divide_fusion.1
  75.5 3.2 %fusion.54 = f32[256,256]{0,1:T(8,128)} fusion(f32[512,256]{1,0:T(8,128)} %reduce-scatter.2.cloned.1.call-done, f32[512]{0:T(512)S(1)} %get-tuple-element.216, f32[512]{0:T(512)S(1)} %get-tuple-element.217), kind=kOutput, calls=%fused_computation.89 | convolution fusion | flops 402915328 | bytes 790528 | tf_op jit(solution)/shard_map/dot_general | solution.py:59
  79.2 39.5 %psum.15 = f32[256]{0:T(256)S(1)} all-reduce(f32[256]{0:T(256)S(1)} %bitcast.108), channel_id=1, replica_groups=mesh['obs'=8,'state'=4] {'obs','state'}, use_global_device_ids=true, to_apply=%region_10.11 | all-reduce | flops 256 | bytes 2048 | tf_op jit(solution)/shard_map/psum | solution.py:64
  118.6 87.0 %all-reduce.3.cloned.1.call-done = f32[256,256]{0,1:T(8,128)} async-done(((f32[256,256]{0,1:T(8,128)}), f32[256,256]{0,1:T(8,128)}) %all-reduce.3.cloned.1.call-update) | async-done | bytes 262160 | tf_op jit(solution)/shard_map/psum | solution.py:64
  205.6 1.0 select_add_fusion.1
  206.7 1.0 fusion.28
  207.7 11.7 %cholesky.49 = f32[128,128]{1,0:T(8,128)S(1)} custom-call(f32[128,128]{1,0:T(8,128)S(1)} %cholesky.115), custom_call_target="Cholesky" | custom-call | tf_op jit(solution)/shard_map/jit(cholesky)/cholesky | solution.py:65
  219.5 9.8 %custom-call.18 = f32[1,128,128]{1,2,0:T(8,128)S(1)} custom-call(f32[1,128,128]{2,1,0:T(8,128)S(1)} %get-tuple-element.214), custom_call_target="InvertDiagBlocksLowerTriangular" | custom-call | tf_op jit(solution)/shard_map/jit(cholesky)/cholesky | solution.py:65
  229.8 11.7 %cholesky.103 = f32[128,128]{1,0:T(8,128)S(1)} custom-call(f32[128,128]{1,0:T(8,128)S(1)} %convolution_subtract_fusion.1), custom_call_target="Cholesky" | custom-call | tf_op jit(solution)/shard_map/jit(cholesky)/cholesky | solution.py:65
  241.9 0.7 compare_reduce_fusion
  244.0 4.3 %while.15 = (s32[]{:T(128)}, f32[256,256]{0,1:T(8,128)S(1)}, s32[2,2]{1,0:T(2,128)S(1)}, f32[2,128,128]{2,1,0:T(8,128)S(1)}, s32[]{:T(128)}) while((s32[]{:T(128)}, f32[256,256]{0,1:T(8,128)S(1)}, s32[2,2]{1,0:T(2,128)S(1)}, f32[2,128,128]{2,1,0:T(8,128)S(1)}, s32[]{:T(128)}) %tuple.58), condition=%wide.while_cond, body=%wide.while_body.sunk | while | flops 2 | bytes 393321 | solution.py:72
  244.0 0.7 fusion.74
  244.6 1.3 dynamic-slice.8
  246.1 0.7 fusion.74
  246.8 1.3 dynamic-slice.8
  248.3 19.9 %custom-call.19 = f32[2,128,128]{1,2,0:T(8,128)S(1)} custom-call(f32[2,128,128]{2,1,0:T(8,128)S(1)} %get-tuple-element.152), custom_call_target="InvertDiagBlocksLowerTriangular" | custom-call | tf_op jit(solution)/shard_map/triangular_solve | solution.py:72
  270.3 1.7 fusion.21
  (52 shorter events, 5.4 us)
Async XLA Ops:
  6.5 66.9 %reduce-scatter.2.cloned.1.call-start = ((), (), s32[]{:S(2)}) async-start(), calls=%async_computation.1 | async-start | bytes 2621440 | tf_op jit(solution)/shard_map/reduce_scatter | solution.py:53
  9.0 3.2 %copy-start.1 = (s32[64]{0:T(128)S(1)}, s32[64]{0:T(128)}, u32[]{:S(2)}) copy-start(s32[64]{0:T(128)} %get-tuple-element.320) | copy-start | bytes 772 | tf_op jit(solution)/shard_map/while
  21.0 3.2 %copy-start.1 = (s32[64]{0:T(128)S(1)}, s32[64]{0:T(128)}, u32[]{:S(2)}) copy-start(s32[64]{0:T(128)} %get-tuple-element.320) | copy-start | bytes 772 | tf_op jit(solution)/shard_map/while
  35.4 170.3 %all-reduce.3.cloned.1.call-start = ((), (), s32[]{:S(2)}) async-start(), calls=%async_computation.2 | async-start | bytes 524288 | tf_op jit(solution)/shard_map/psum | solution.py:64
  73.4 5.3 %copy-start = (f32[512,256]{1,0:T(8,128)S(1)}, f32[512,256]{1,0:T(8,128)}, u32[]{:S(2)}) copy-start(f32[512,256]{1,0:T(8,128)} %reduce-scatter.2.cloned.1.call-done) | copy-start | bytes 1572868
Sparse Core Ops, SparseCore 0:
  35.5 37.9 reduce-scatter.1
  78.9 126.6 all-reduce.2
where the time goes:
time: 280 us; the launch traced here: 279 us
  waiting for transfers between devices  124 us (44%)
  other arithmetic  61.7 us (22%)
  blocking collectives  39.5 us (14%)
  matrix products  26.2 us (9%)
  between operations  14.9 us (5%)
  local copies, waits for them, and re-layouts  12.4 us (4%)
    psum x1, waiting for transfers between devices, on_device(): lax.psum((gram_part, projected_part), ('obs', 'state'))  87 us
    psum x1, blocking collectives, on_device(): lax.psum((gram_part, projected_part), ('obs', 'state'))  39.5 us
    reduce_scatter x1, waiting for transfers between devices, on_device(): lax.psum_scatter(slab_term, 'state', scatter_dimension=0, tiled=True)  37 us
    another operation x6, other arithmetic, on_device(): lower_factor = jnp.linalg.cholesky(gram_sum + (K - 1) * identity)  34 us
    another operation x3, other arithmetic, on_device(): lax.linalg.triangular_solve(lower_factor, identity, left_side=True, lower...  19.9 us
    dot_general x2, matrix products, add_group(): jnp.einsum('mb,bik->mik', onehot, upper_part, preferred_element_type=jnp....  9.29 us
    dot_general x2, matrix products, add_group(): jnp.einsum('bij,bjk->bik', blocks, picked, preferred_element_type=jnp.flo...  6.45 us
  transfers between devices with their start and end apart: 2, of which 2 were waited for; matrix products, arithmetic and copies ran while one was open for 1% of the time, Pallas kernels for 0%

commit v1 on v0

--- a/solution.py
+++ b/solution.py
@@ -8,6 +8,12 @@
 BS = 128
 M_DEV = 2048
 BLK_DEV = 64
+
+
+def recast_skins_on_mesh(xs):
+    for i in ("obs", "state"):
+        xs = lax.psum(xs, axis_name=i)
+    return xs
 
 
 def on_device(ensemble, obs_values, obs_error, h_blocks, block_rows, block_cols, block_count):
@@ -61,7 +67,7 @@
     )
     projected_part = jnp.dot(innovation, whitened, precision=lax.Precision.HIGHEST)
     identity = jnp.eye(K, dtype=jnp.float32)
-    gram_sum, projected_innovation = lax.psum((gram_part, projected_part), ("obs", "state"))
+    gram_sum, projected_innovation = recast_skins_on_mesh((gram_part, projected_part))
     lower_factor = jnp.linalg.cholesky(gram_sum + (K - 1) * identity)
     halfway = lax.linalg.triangular_solve(
         lower_factor, projected_innovation[:, None], left_side=True, lower=True

time: 280 us -> 253 us (0.904)
  blocking collectives: 39.5 us -> 23.7 us
  waiting for transfers between devices: 124 us -> 113 us
    psum x1 -> x2, blocking collectives: 39.5 us -> 23.7 us  [recast_skins_on_mesh(): xs = lax.psum(xs, axis_name=i)]
    psum x1 -> x2, waiting for transfers between devices: 87 us -> 76.3 us  [recast_skins_on_mesh(): xs = lax.psum(xs, axis_name=i)]
  transfers between devices with their start and end apart: 2 -> 3, of which waited for: 2 -> 3; matrix products, arithmetic and copies ran while one was open for 1% -> 1% of each run, Pallas kernels for 0% -> 0%
where the time goes in v1:
time: 253 us; the launch traced here: 252 us
  waiting for transfers between devices  113 us (45%)
  other arithmetic  61.7 us (24%)
  matrix products  26.2 us (10%)
  blocking collectives  23.7 us (9%)
  between operations  14.6 us (6%)
  local copies, waits for them, and re-layouts  12.4 us (5%)
    psum x2, waiting for transfers between devices, recast_skins_on_mesh(): xs = lax.psum(xs, axis_name=i)  76.3 us
    reduce_scatter x1, waiting for transfers between devices, on_device(): lax.psum_scatter(slab_term, 'state', scatter_dimension=0, tiled=True)  37.1 us
    another operation x6, other arithmetic, on_device(): lower_factor = jnp.linalg.cholesky(gram_sum + (K - 1) * identity)  34 us
    psum x2, blocking collectives, recast_skins_on_mesh(): xs = lax.psum(xs, axis_name=i)  23.7 us
    another operation x3, other arithmetic, on_device(): lax.linalg.triangular_solve(lower_factor, identity, left_side=True, lower...  19.9 us
    dot_general x2, matrix products, add_group(): jnp.einsum('mb,bik->mik', onehot, upper_part, preferred_element_type=jnp....  9.29 us
    dot_general x2, matrix products, add_group(): jnp.einsum('bij,bjk->bik', blocks, picked, preferred_element_type=jnp.flo...  6.45 us
  transfers between devices with their start and end apart: 3, of which 3 were waited for; matrix products, arithmetic and copies ran while one was open for 1% of the time, Pallas kernels for 0%

profile of v1, /device:TPU:0, one launch (start us, length us, event | category | flops | bytes accessed | tf_op | source)
XLA Modules:
  0.0 252.3 jit_solution(18180711492368565137)
XLA Ops:
  6.5 24.7 %while.16 = (s32[]{:T(128)}, f32[16,128,256]{2,0,1:T(8,128)}, s32[64]{0:T(128)}, s32[]{:T(128)}, bf16[64,128,128]{2,1,0:T(8,128)(2,1)}, /*index=5*/s32[64]{0:T(1...) while((s32[]{:T(128)}, f32[16,128,256]{2,0,1:T(8,128)}, ...), condition=%wide.region_2.0_spmd.clone, body=%wide.region_1.0_spmd.clone.sunk | while | flops 341314720 | bytes 24123700 | solution.py:52
  6.5 0.7 compare_select_fusion.2
  7.3 1.7 gather_fusion
  9.0 3.2 %subtract_convert_fusion.2 = (bf16[32,128,256]{2,1,0:T(8,128)(2,1)S(1)}, bf16[32,128,256]{2,1,0:T(8,128)(2,1)}) fusion(bf16[32,128,256]{2,1,0:T(8,128)(2,1)S(1)} %gather_fusion, bf16[64,128,128]{2,1,0:T(8,128)(2,1)} %get-tuple-element.322, s32[]{:T(128)S(6)} %select_n.37), kind=kOutput, calls=%fused_computation.4.clone.1 | convolution fusion | flops 272629760 | bytes 7340036 | tf_op jit(solution)/shard_map/while/body/eval_jaxpr/bij,bjk->bik/dot_general | solution.py:40
  13.0 1.3 fusion.80
  14.2 4.3 %fusion.81 = f32[16,128,256]{2,0,1:T(8,128)} fusion(f32[16,128,256]{2,0,1:T(8,128)S(1)} %fusion.80, f32[16,128,256]{2,0,1:T(8,128)} %get-tuple-element.308, bf16[32,128,256]{2,1,0:T(8,128)(2,1)} %get-tuple-element.295, pred[]{:T(512)S(6)} %compare.30, s32[32]{0:T(128)S(1)} %dynamic_slice.54, pred[32]{0:T(512)(128)(4,1)S(1)} %add_compare_fusion.2), kind=kOutput, calls=%fused_computation.10.clone.1 | convolution fusion | flops 35128320 | bytes 8388769 | tf_op jit(solution)/shard_map/while/body/eval_jaxpr/mb,bik->mik/dot_general | solution.py:44
  18.6 0.7 compare_select_fusion.2
  19.3 1.7 gather_fusion
  21.0 3.2 %subtract_convert_fusion.2 = (bf16[32,128,256]{2,1,0:T(8,128)(2,1)S(1)}, bf16[32,128,256]{2,1,0:T(8,128)(2,1)}) fusion(bf16[32,128,256]{2,1,0:T(8,128)(2,1)S(1)} %gather_fusion, bf16[64,128,128]{2,1,0:T(8,128)(2,1)} %get-tuple-element.322, s32[]{:T(128)S(6)} %select_n.37), kind=kOutput, calls=%fused_computation.4.clone.1 | convolution fusion | flops 272629760 | bytes 7340036 | tf_op jit(solution)/shard_map/while/body/eval_jaxpr/bij,bjk->bik/dot_general | solution.py:40
  25.0 1.3 fusion.80
  26.3 5.0 %fusion.81 = f32[16,128,256]{2,0,1:T(8,128)} fusion(f32[16,128,256]{2,0,1:T(8,128)S(1)} %fusion.80, f32[16,128,256]{2,0,1:T(8,128)} %get-tuple-element.308, bf16[32,128,256]{2,1,0:T(8,128)(2,1)} %get-tuple-element.295, pred[]{:T(512)S(6)} %compare.30, s32[32]{0:T(128)S(1)} %dynamic_slice.54, pred[32]{0:T(512)(128)(4,1)S(1)} %add_compare_fusion.2), kind=kOutput, calls=%fused_computation.10.clone.1 | convolution fusion | flops 35128320 | bytes 8388769 | tf_op jit(solution)/shard_map/while/body/eval_jaxpr/mb,bik->mik/dot_general | solution.py:44
  31.2 4.1 %copy.18 = f32[16,128,256]{2,1,0:T(8,128)} copy(f32[16,128,256]{2,0,1:T(8,128)} %get-tuple-element.144) | data formatting | bytes 4194304 | tf_op jit(solution)/shard_map/while | solution.py:52
  35.4 0.9 convert_reduce_fusion
  36.4 37.1 %reduce-scatter.2.cloned.1.call-done = f32[512,256]{1,0:T(8,128)} async-done(((f32[2048,256]{1,0:T(8,128)}), f32[512,256]{1,0:T(8,128)}) %reduce-scatter.2.cloned.1.call-update) | async-done | bytes 524304 | tf_op jit(solution)/shard_map/reduce_scatter | solution.py:59
  73.4 1.3 reduce_sum.19
  74.7 0.8 subtract_divide_fusion.1
  75.5 3.2 %fusion.54 = f32[256,256]{0,1:T(8,128)} fusion(f32[512,256]{1,0:T(8,128)} %reduce-scatter.2.cloned.1.call-done, f32[512]{0:T(512)S(1)} %get-tuple-element.216, f32[512]{0:T(512)S(1)} %get-tuple-element.217), kind=kOutput, calls=%fused_computation.89 | convolution fusion | flops 402915328 | bytes 790528 | tf_op jit(solution)/shard_map/dot_general | solution.py:65
  78.8 55.5 %all-reduce.4.cloned.1.call-done = f32[256,256]{0,1:T(8,128)} async-done(((f32[256,256]{0,1:T(8,128)}), f32[256,256]{0,1:T(8,128)}) %all-reduce.4.cloned.1.call-update) | async-done | bytes 262160 | tf_op jit(solution)/shard_map/psum | solution.py:15
  134.8 13.7 %psum.30 = f32[256]{0:T(256)S(1)} all-reduce(f32[256]{0:T(256)S(1)} %bitcast.108), channel_id=1, replica_groups=mesh['obs'=8,'state'=4] {'obs'}, use_global_device_ids=true, to_apply=%region_11.12 | all-reduce | flops 256 | bytes 2048 | tf_op jit(solution)/shard_map/psum | solution.py:15
  148.5 10.0 %psum.31 = f32[256]{0:T(256)S(1)} all-reduce(f32[256]{0:T(256)S(1)} %psum.30), channel_id=1, replica_groups=mesh['obs'=8,'state'=4] {'state'}, use_global_device_ids=true, to_apply=%region_12.13 | all-reduce | flops 256 | bytes 2048 | tf_op jit(solution)/shard_map/psum | solution.py:15
  158.5 20.9 %all-reduce.6.cloned.1.call-done = f32[256,256]{0,1:T(8,128)} async-done(((f32[256,256]{0,1:T(8,128)}), f32[256,256]{0,1:T(8,128)}) %all-reduce.6.cloned.1.call-update) | async-done | bytes 262160 | tf_op jit(solution)/shard_map/psum | solution.py:15
  179.3 1.0 select_add_fusion.1
  180.4 1.0 fusion.28
  181.5 11.7 %cholesky.49 = f32[128,128]{1,0:T(8,128)S(1)} custom-call(f32[128,128]{1,0:T(8,128)S(1)} %cholesky.115), custom_call_target="Cholesky" | custom-call | tf_op jit(solution)/shard_map/jit(cholesky)/cholesky | solution.py:71
  193.2 9.8 %custom-call.18 = f32[1,128,128]{1,2,0:T(8,128)S(1)} custom-call(f32[1,128,128]{2,1,0:T(8,128)S(1)} %get-tuple-element.214), custom_call_target="InvertDiagBlocksLowerTriangular" | custom-call | tf_op jit(solution)/shard_map/jit(cholesky)/cholesky | solution.py:71
  203.5 11.7 %cholesky.103 = f32[128,128]{1,0:T(8,128)S(1)} custom-call(f32[128,128]{1,0:T(8,128)S(1)} %convolution_subtract_fusion.1), custom_call_target="Cholesky" | custom-call | tf_op jit(solution)/shard_map/jit(cholesky)/cholesky | solution.py:71
  215.6 0.7 compare_reduce_fusion
  217.7 4.3 %while.15 = (s32[]{:T(128)}, f32[256,256]{0,1:T(8,128)S(1)}, s32[2,2]{1,0:T(2,128)S(1)}, f32[2,128,128]{2,1,0:T(8,128)S(1)}, s32[]{:T(128)}) while((s32[]{:T(128)}, f32[256,256]{0,1:T(8,128)S(1)}, s32[2,2]{1,0:T(2,128)S(1)}, f32[2,128,128]{2,1,0:T(8,128)S(1)}, s32[]{:T(128)}) %tuple.58), condition=%wide.while_cond, body=%wide.while_body.sunk | while | flops 2 | bytes 393321 | solution.py:78
  218.4 1.3 dynamic-slice.8
  220.5 1.3 dynamic-slice.8
  222.0 19.9 %custom-call.19 = f32[2,128,128]{1,2,0:T(8,128)S(1)} custom-call(f32[2,128,128]{2,1,0:T(8,128)S(1)} %get-tuple-element.152), custom_call_target="InvertDiagBlocksLowerTriangular" | custom-call | tf_op jit(solution)/shard_map/triangular_solve | solution.py:78
  244.0 1.7 fusion.21
  (56 shorter events, 6.8 us)
Async XLA Ops:
  6.5 66.9 %reduce-scatter.2.cloned.1.call-start = ((), (), s32[]{:S(2)}) async-start(), calls=%async_computation.1 | async-start | bytes 2621440 | tf_op jit(solution)/shard_map/reduce_scatter | solution.py:59
  9.0 3.2 %copy-start.1 = (s32[64]{0:T(128)S(1)}, s32[64]{0:T(128)}, u32[]{:S(2)}) copy-start(s32[64]{0:T(128)} %get-tuple-element.320) | copy-start | bytes 772 | tf_op jit(solution)/shard_map/while
  21.0 3.2 %copy-start.1 = (s32[64]{0:T(128)S(1)}, s32[64]{0:T(128)}, u32[]{:S(2)}) copy-start(s32[64]{0:T(128)} %get-tuple-element.320) | copy-start | bytes 772 | tf_op jit(solution)/shard_map/while
  35.4 98.9 %all-reduce.4.cloned.1.call-start = ((), (), s32[]{:S(2)}) async-start(), calls=%async_computation.2 | async-start | bytes 524288 | tf_op jit(solution)/shard_map/psum | solution.py:15
  73.4 60.9 %copy-start = (f32[512,256]{1,0:T(8,128)S(1)}, f32[512,256]{1,0:T(8,128)}, u32[]{:S(2)}) copy-start(f32[512,256]{1,0:T(8,128)} %reduce-scatter.2.cloned.1.call-done) | copy-start | bytes 1572868
  78.7 100.6 %all-reduce.6.cloned.1.call-start = ((), (), s32[]{:S(2)}) async-start(), calls=%async_computation.3 | async-start | bytes 524288 | tf_op jit(solution)/shard_map/psum | solution.py:15
Sparse Core Ops, SparseCore 0:
  35.5 37.9 reduce-scatter.1
  78.9 55.3 all-reduce.3
  137.2 42.0 all-reduce.5
